TPU v7x, 256 devices: a whole 4x4x8 slice. The times are simulated.
256 devices in a mesh: row: 32 (over z, y), col: 8 (over x, core).
Axes of the slice: x: 4, y: 4, z: 8, core: 2. Of those that a mesh axis runs over, the one named last changes fastest.
Arguments:
- embeddings: bfloat16 [262144, 1024], P('row', 'col'), may hold values from -0.1875 to 0.1875
- quality: float32 [262144], P('row'), may hold values from 0.5 to 2
- probes: float32 [32, 262144], P(None, 'row'), may hold values from -6 to 6
- neighbors: int32 [2048, 8], P('row'), may hold values from 0 to 2047, as said below
Outputs:
- first: float32 [32, 262144], P(None, 'row')
- second: float32 [32, 262144], P(None, 'row')
Inputs may be any that keep to these rules, and one draw needn't show every extreme that they name: `neighbors`: block b is held by row index b // 64. Among the 512 entries of one row index's blocks, at most 8 name blocks of any one other row index, and on every row index some other index is named exactly 8 times; the remaining entries name the index's own blocks.
All inputs are finite; a program needn't handle non-finite values.
Results may differ from a plain program's by a relative error of at most 0.02.
Values may be sent and summed in bfloat16 or wider, within the bound.
A program may use at most 64 MiB of HBM per device.

v0:
```python
import jax
import jax.numpy as jnp
from jax import lax
from jax.sharding import PartitionSpec as P


def body(embeddings, quality, probes, neighbors):
    nrow = lax.axis_size("row")
    myself = lax.axis_index("row")
    blk_count, list_len = neighbors.shape
    docs, width = embeddings.shape
    block_len = docs // blk_count
    nprobe = probes.shape[0]
    slots = max(2, blk_count * list_len // (2 * nrow))
    blocked = embeddings.reshape(blk_count, block_len, width)
    flat = neighbors.reshape(-1)
    owner = flat // blk_count
    local = flat % blk_count
    remote = owner != myself
    onehot = (owner[:, None] == jnp.arange(nrow, dtype=jnp.int32)[None, :]).astype(jnp.int32)
    slot = jnp.sum((jnp.cumsum(onehot, axis=0) - onehot) * onehot, axis=1)
    request = jnp.zeros((nrow, slots), jnp.int32)
    request = request.at[jnp.where(remote, owner, nrow), slot].set(local, mode="drop")
    wanted = lax.all_to_all(request, "row", split_axis=0, concat_axis=0, tiled=True)
    source = jnp.where(remote, blk_count + owner * slots + slot, local)

    def apply(vec):
        scaled = (vec * quality[None, :]).astype(jnp.bfloat16).reshape(nprobe, blk_count, block_len)
        own = jnp.einsum(
            "bdc,pbd->bcp", blocked, scaled, preferred_element_type=jnp.float32
        ).astype(jnp.bfloat16)
        outgoing = own.reshape(blk_count, width * nprobe)[wanted]
        arrived = lax.all_to_all(outgoing, "row", split_axis=0, concat_axis=0, tiled=True)
        table = jnp.concatenate([own, arrived.reshape(nrow * slots, width, nprobe)], axis=0)
        gathered = table[source].reshape(blk_count, list_len, width, nprobe)
        summed = jnp.sum(gathered, axis=1, dtype=jnp.float32).astype(jnp.bfloat16)
        partial_value = jnp.einsum(
            "bdc,bcp->pbd", blocked, summed, preferred_element_type=jnp.float32
        ).reshape(nprobe, docs)
        total = lax.psum(partial_value.astype(jnp.bfloat16), "col").astype(jnp.float32)
        return total * quality[None, :] - vec

    first = apply(probes)
    second = 2.0 * apply(first) - probes
    return (first, second)


def solution(mesh):
    placed = (P("row", "col"), P("row"), P(None, "row"), P("row", None))
    return jax.shard_map(
        body,
        mesh=mesh,
        in_specs=placed,
        out_specs=(P(None, "row"), P(None, "row")),
        check_vma=False,
    )
```

profile of v0, /device:TPU:8, one launch (start us, length us, event | category | flops | bytes accessed | tf_op | source)
XLA Modules:
  0.0 380.9 jit_solution(4146133513576657002)
XLA Ops:
  10.1 22.3 %scatter_fusion = s32[32,8]{0,1:T(8,128)S(1)} fusion(s32[32,8]{0,1:T(8,128)S(1)} %broadcast.250, s32[512]{0:T(512)S(1)} %bitcast.75, s32[512]{0:T(512)S(1)} %get-tuple-element.6), kind=kCustom, calls=%fused_computation.4 | custom fusion | bytes 10240 | tf_op jit(solution)/shard_map/scatter | solution.py:23
  33.0 11.7 %all-to-all-start = ((s32[32,1,8]{2,1,0:T(1,128)}), s32[32,1,8]{2,1,0:T(1,128)S(1)}, u32[]{:S(2)}, u32[]{:S(2)}) async-start(s32[32,1,8]{2,1,0:T(1,128)} %copy.31), calls=%async_computation | async-start | bytes 32768 | tf_op jit(solution)/shard_map/all_to_all | solution.py:24
  46.2 3.7 copy.26
  51.5 1.8 all-to-all-done
  53.4 3.2 gather_fusion
  56.6 8.0 %all-to-all-start.1 = ((bf16[32,8,4096]{2,1,0:T(8,128)(2,1)}), bf16[32,8,4096]{2,1,0:T(8,128)(2,1)}, u32[]{:S(2)}, u32[]{:S(2)}) async-start(bf16[32,8,4096]{2,1,0:T(8,128)(2,1)} %bitcast.76), calls=%async_computation.1 | async-start | bytes 4194304 | tf_op jit(solution)/shard_map/all_to_all | solution.py:33
  64.7 48.8 %all-to-all-done.1 = bf16[32,8,4096]{2,1,0:T(8,128)(2,1)} async-done(((bf16[32,8,4096]{2,1,0:T(8,128)(2,1)}), bf16[32,8,4096]{2,1,0:T(8,128)(2,1)}, u32[]{:S(2)}, u32[]{:S(2)}) %all-to-all-start.1) | async-done | bytes 2097184 | tf_op jit(solution)/shard_map/all_to_all | solution.py:33
  113.5 9.4 %reshape.270 = bf16[256,128,32]{2,1,0:T(8,128)(2,1)} reshape(bf16[32,8,4096]{2,1,0:T(8,128)(2,1)} %all-to-all-done.1) | data formatting | bytes 4194304 | tf_op jit(solution)/shard_map/reshape | solution.py:34
  122.8 8.0 %copy.33 = bf16[256,128,32]{1,2,0:T(8,128)(2,1)} copy(bf16[256,128,32]{2,1,0:T(8,128)(2,1)} %reshape.270) | data formatting | bytes 4194304 | tf_op jit(solution)/shard_map/reshape | solution.py:34
  130.8 3.3 pad_maximum_fusion
  134.1 4.9 %gather_fusion.1 = bf16[512,128,32]{1,2,0:T(8,128)(2,1)} fusion(bf16[320,128,32]{1,2,0:T(8,128)(2,1)} %pad_maximum_fusion, s32[1024]{0:T(1024)S(1)} %pad_clamp_fusion), kind=kCustom, calls=%fused_computation.1 | custom fusion | bytes 8390656 | tf_op jit(solution)/shard_map/gather | solution.py:35
  139.0 3.1 bitcast_reduce_fusion.1
  144.5 63.9 %all-reduce.3.cloned.1.call-done = bf16[32,8192]{1,0:T(8,128)(2,1)} async-done(((bf16[32,8192]{1,0:T(8,128)(2,1)}), bf16[32,8192]{1,0:T(8,128)(2,1)}) %all-reduce.3.cloned.1.call-update) | async-done | bytes 524304 | tf_op jit(solution)/shard_map/psum | solution.py:40
  208.4 2.2 fusion.5
  211.3 2.6 copy.38
  215.4 3.2 gather_fusion.2
  218.7 58.7 %all_to_all.22 = bf16[32,8,4096]{2,1,0:T(8,128)(2,1)} all-to-all(bf16[32,8,4096]{2,1,0:T(8,128)(2,1)} %bitcast.77), channel_id=1, replica_groups=mesh['row'=32,'col'=8] {'row'}, dimensions={0} | all-to-all | bytes 4194304 | tf_op jit(solution)/shard_map/all_to_all | solution.py:33
  277.3 9.4 %reshape.274 = bf16[256,128,32]{2,1,0:T(8,128)(2,1)} reshape(bf16[32,8,4096]{2,1,0:T(8,128)(2,1)} %all_to_all.22) | data formatting | bytes 4194304 | tf_op jit(solution)/shard_map/reshape | solution.py:34
  286.7 7.9 %copy.40 = bf16[256,128,32]{1,2,0:T(8,128)(2,1)} copy(bf16[256,128,32]{2,1,0:T(8,128)(2,1)} %reshape.274) | data formatting | bytes 4194304 | tf_op jit(solution)/shard_map/reshape | solution.py:34
  294.6 3.3 pad_maximum_fusion.1
  298.0 4.9 %gather_fusion.3 = bf16[512,128,32]{1,2,0:T(8,128)(2,1)} fusion(bf16[320,128,32]{1,2,0:T(8,128)(2,1)} %pad_maximum_fusion.1, s32[1024]{0:T(1024)S(1)} %pad_clamp_fusion), kind=kCustom, calls=%fused_computation.3 | custom fusion | bytes 8390656 | tf_op jit(solution)/shard_map/gather | solution.py:35
  302.8 3.1 bitcast_reduce_fusion
  308.1 63.5 %all-reduce.5.cloned.1.call-done = bf16[32,8192]{1,0:T(8,128)(2,1)} async-done(((bf16[32,8192]{1,0:T(8,128)(2,1)}), bf16[32,8192]{1,0:T(8,128)(2,1)}) %all-reduce.5.cloned.1.call-update) | async-done | bytes 524304 | tf_op jit(solution)/shard_map/psum | solution.py:40
  371.5 2.5 multiply_subtract_fusion
  (44 shorter events, 13.3 us)
Async XLA Ops:
  7.2 37.5 %copy-start = (bf16[8192,128]{1,0:T(8,128)(2,1)S(1)}, bf16[8192,128]{1,0:T(8,128)(2,1)}, u32[]{:S(2)}) copy-start(bf16[8192,128]{1,0:T(8,128)(2,1)} %param.4) | copy-start | bytes 6291460
  10.0 34.7 %copy-start.1 = (f32[32,8192]{1,0:T(8,128)S(1)}, f32[32,8192]{1,0:T(8,128)}, u32[]{:S(2)}) copy-start(f32[32,8192]{1,0:T(8,128)} %param.6) | copy-start | bytes 3145732
  10.1 34.7 %copy-start.5 = (f32[8192]{0:T(1024)S(1)}, f32[8192]{0:T(1024)}, u32[]{:S(2)}) copy-start(f32[8192]{0:T(1024)} %param.5) | copy-start | bytes 98308
  33.0 20.3 %all-to-all-start = ((s32[32,1,8]{2,1,0:T(1,128)}), s32[32,1,8]{2,1,0:T(1,128)S(1)}, u32[]{:S(2)}, u32[]{:S(2)}) async-start(s32[32,1,8]{2,1,0:T(1,128)} %copy.31), calls=%async_computation | async-start | bytes 32768 | tf_op jit(solution)/shard_map/all_to_all | solution.py:24
  56.6 56.9 %all-to-all-start.1 = ((bf16[32,8,4096]{2,1,0:T(8,128)(2,1)}), bf16[32,8,4096]{2,1,0:T(8,128)(2,1)}, u32[]{:S(2)}, u32[]{:S(2)}) async-start(bf16[32,8,4096]{2,1,0:T(8,128)(2,1)} %bitcast.76), calls=%async_computation.1 | async-start | bytes 4194304 | tf_op jit(solution)/shard_map/all_to_all | solution.py:33
  64.6 143.8 %all-reduce.3.cloned.1.call-start = ((), (), s32[]{:S(2)}) async-start(), calls=%async_computation.3 | async-start | bytes 1048576 | tf_op jit(solution)/shard_map/psum | solution.py:40
  122.8 8.0 %copy-start.4 = (bf16[64,128,32]{1,2,0:T(8,128)(2,1)S(1)}, bf16[64,128,32]{1,2,0:T(8,128)(2,1)}, u32[]{:S(2)}) copy-start(bf16[64,128,32]{1,2,0:T(8,128)(2,1)} %fusion) | copy-start | bytes 1572868
  142.1 66.3 %copy-start.2 = (f32[32,8192]{1,0:T(8,128)S(1)}, f32[32,8192]{1,0:T(8,128)}, u32[]{:S(2)}) copy-start(f32[32,8192]{1,0:T(8,128)} %param.6) | copy-start | bytes 3145732
  144.3 227.3 %all-reduce.5.cloned.1.call-start = ((), (), s32[]{:S(2)}) async-start(), calls=%async_computation.4 | async-start | bytes 1048576 | tf_op jit(solution)/shard_map/psum | solution.py:40
  306.0 65.6 %copy-start.3 = (f32[32,8192]{1,0:T(8,128)S(1)}, f32[32,8192]{1,0:T(8,128)}, u32[]{:S(2)}) copy-start(f32[32,8192]{1,0:T(8,128)} %param.6) | copy-start | bytes 3145732
Sparse Core Ops, SparseCore 0:
  144.4 64.0 all-reduce.2
  308.2 63.2 all-reduce.4
where the time goes:
time: 382 us; the launch traced here: 381 us
  waiting for transfers between devices  178 us (47%)
  local copies, waits for them, and re-layouts  86.4 us (23%)
  blocking collectives  58.7 us (15%)
  starting transfers between devices  20 us (5%)
  other arithmetic  19 us (5%)
  between operations  14.2 us (4%)
  matrix products  4.49 us (1%)
    psum x2, waiting for transfers between devices, apply(): lax.psum(partial_value.astype(jnp.bfloat16), 'col').astype(jnp.float32)  127 us
    all_to_all x1, blocking collectives, apply(): lax.all_to_all(outgoing, 'row', split_axis=0, concat_axis=0, tiled=True)  58.7 us
    all_to_all x1, waiting for transfers between devices, apply(): lax.all_to_all(outgoing, 'row', split_axis=0, concat_axis=0, tiled=True)  48.8 us
    reshape x4, local copies, waits for them, and re-layouts, apply(): arrived.reshape(nrow * slots, width, nprobe)  34.6 us
    scatter x1, local copies, waits for them, and re-layouts, body(): request.at[jnp.where(remote, owner, nrow), slot].set(local, mode='drop')  22.3 us
    all_to_all x1, starting transfers between devices, body(): lax.all_to_all(request, 'row', split_axis=0, concat_axis=0, tiled=True)  11.7 us
    gather x2, local copies, waits for them, and re-layouts, apply(): gathered = table[source].reshape(blk_count, list_len, width, nprobe)  9.75 us
    unnamed x3, other arithmetic  8.43 us
  transfers between devices with their start and end apart: 4, of which 4 were waited for; matrix products, arithmetic and copies ran while one was open for 2% of the time, Pallas kernels for 0%

commit v1 on v0

--- a/solution.py
+++ b/solution.py
@@ -37,7 +37,9 @@
         partial_value = jnp.einsum(
             "bdc,bcp->pbd", blocked, summed, preferred_element_type=jnp.float32
         ).reshape(nprobe, docs)
-        total = lax.psum(partial_value.astype(jnp.bfloat16), "col").astype(jnp.float32)
+        total = jnp.sum(lax.all_gather(partial_value.astype(jnp.bfloat16), "col"), axis=0).astype(
+            jnp.float32
+        )
         return total * quality[None, :] - vec
 
     first = apply(probes)

time: 382 us -> 329 us (0.86)
  waiting for transfers between devices: 178 us -> 113 us
  other arithmetic: 19 us -> 26.5 us
    psum x2 -> x0, waiting for transfers between devices: 127 us -> none  [apply(): lax.psum(partial_value.astype(jnp.bfloat16), 'col').astype(jnp.float32)]
    all_gather x0 -> x2, waiting for transfers between devices: none -> 62.5 us  [apply(): lax.all_gather(partial_value.astype(jnp.bfloat16), 'col')]
    reduce_sum x0 -> x2, other arithmetic: none -> 7.45 us  [apply(): jnp.sum(lax.all_gather(partial_value.astype(jnp.bfloat16), 'col'), axis=0)]
where the time goes in v1:
time: 329 us; the launch traced here: 327 us
  waiting for transfers between devices  113 us (34%)
  local copies, waits for them, and re-layouts  87.1 us (26%)
  blocking collectives  61.2 us (19%)
  other arithmetic  26.5 us (8%)
  starting transfers between devices  20 us (6%)
  between operations  14.3 us (4%)
  matrix products  4.49 us (1%)
    all_gather x2, waiting for transfers between devices, apply(): lax.all_gather(partial_value.astype(jnp.bfloat16), 'col')  62.5 us
    all_to_all x1, blocking collectives, apply(): lax.all_to_all(outgoing, 'row', split_axis=0, concat_axis=0, tiled=True)  61.2 us
    all_to_all x1, waiting for transfers between devices, apply(): lax.all_to_all(outgoing, 'row', split_axis=0, concat_axis=0, tiled=True)  48.8 us
    reshape x4, local copies, waits for them, and re-layouts, apply(): arrived.reshape(nrow * slots, width, nprobe)  34.6 us
    scatter x1, local copies, waits for them, and re-layouts, body(): request.at[jnp.where(remote, owner, nrow), slot].set(local, mode='drop')  22.3 us
    all_to_all x1, starting transfers between devices, body(): lax.all_to_all(request, 'row', split_axis=0, concat_axis=0, tiled=True)  11.7 us
    gather x2, local copies, waits for them, and re-layouts, apply(): gathered = table[source].reshape(blk_count, list_len, width, nprobe)  9.75 us
    unnamed x3, other arithmetic  8.43 us
  transfers between devices with their start and end apart: 4, of which 4 were waited for; matrix products, arithmetic and copies ran while one was open for 2% of the time, Pallas kernels for 0%

profile of v1, /device:TPU:8, one launch (start us, length us, event | category | flops | bytes accessed | tf_op | source)
XLA Modules:
  0.0 326.7 jit_solution(5274161740040469022)
XLA Ops:
  10.1 22.3 %scatter_fusion = s32[32,8]{0,1:T(8,128)S(1)} fusion(s32[32,8]{0,1:T(8,128)S(1)} %broadcast.250, s32[512]{0:T(512)S(1)} %bitcast.67, s32[512]{0:T(512)S(1)} %get-tuple-element.6), kind=kCustom, calls=%fused_computation.4 | custom fusion | bytes 10240 | tf_op jit(solution)/shard_map/scatter | solution.py:23
  33.0 11.7 %all-to-all-start = ((s32[32,1,8]{2,1,0:T(1,128)}), s32[32,1,8]{2,1,0:T(1,128)S(1)}, u32[]{:S(2)}, u32[]{:S(2)}) async-start(s32[32,1,8]{2,1,0:T(1,128)} %copy.31), calls=%async_computation | async-start | bytes 32768 | tf_op jit(solution)/shard_map/all_to_all | solution.py:24
  46.2 3.7 %copy.26 = bf16[64,128,32]{0,2,1:T(8,128)(2,1)} copy(bf16[64,128,32]{1,2,0:T(8,128)(2,1)} %fusion) | data formatting | bytes 1048576 | tf_op jit(solution)/shard_map/convert_element_type | solution.py:31
  53.4 3.2 gather_fusion
  56.6 8.0 %all-to-all-start.1 = ((bf16[32,8,4096]{2,1,0:T(8,128)(2,1)}), bf16[32,8,4096]{2,1,0:T(8,128)(2,1)}, u32[]{:S(2)}, u32[]{:S(2)}) async-start(bf16[32,8,4096]{2,1,0:T(8,128)(2,1)} %bitcast.68), calls=%async_computation.1 | async-start | bytes 4194304 | tf_op jit(solution)/shard_map/all_to_all | solution.py:33
  64.7 48.8 %all-to-all-done.1 = bf16[32,8,4096]{2,1,0:T(8,128)(2,1)} async-done(((bf16[32,8,4096]{2,1,0:T(8,128)(2,1)}), bf16[32,8,4096]{2,1,0:T(8,128)(2,1)}, u32[]{:S(2)}, u32[]{:S(2)}) %all-to-all-start.1) | async-done | bytes 2097184 | tf_op jit(solution)/shard_map/all_to_all | solution.py:33
  113.5 9.4 %reshape.290 = bf16[256,128,32]{2,1,0:T(8,128)(2,1)} reshape(bf16[32,8,4096]{2,1,0:T(8,128)(2,1)} %all-to-all-done.1) | data formatting | bytes 4194304 | tf_op jit(solution)/shard_map/reshape | solution.py:34
  122.8 8.0 %copy.33 = bf16[256,128,32]{1,2,0:T(8,128)(2,1)} copy(bf16[256,128,32]{2,1,0:T(8,128)(2,1)} %reshape.290) | data formatting | bytes 4194304 | tf_op jit(solution)/shard_map/reshape | solution.py:34
  130.8 3.3 %pad_maximum_fusion = bf16[320,128,32]{1,2,0:T(8,128)(2,1)} fusion(bf16[256,128,32]{1,2,0:T(8,128)(2,1)} %copy.33, bf16[64,128,32]{1,2,0:T(8,128)(2,1)S(1)} %copy-done.4), kind=kLoop, calls=%fused_computation.7 | loop fusion | flops 1310720 | bytes 5242880 | tf_op jit(solution)/shard_map/concatenate | solution.py:34
  134.1 4.9 %gather_fusion.1 = bf16[512,128,32]{1,2,0:T(8,128)(2,1)} fusion(bf16[320,128,32]{1,2,0:T(8,128)(2,1)} %pad_maximum_fusion, s32[1024]{0:T(1024)S(1)} %pad_clamp_fusion), kind=kCustom, calls=%fused_computation.1 | custom fusion | bytes 8390656 | tf_op jit(solution)/shard_map/gather | solution.py:35
  139.0 3.1 bitcast_reduce_fusion.1
  144.8 32.4 %all-gather.3.cloned.1.call-done = bf16[8,32,8192]{2,1,0:T(8,128)(2,1)} async-done(((bf16[1,32,8192]{2,1,0:T(8,128)(2,1)}), bf16[8,32,8192]{2,1,0:T(8,128)(2,1)}) %all-gather.3.cloned.1.call-update) | async-done | bytes 4194320 | tf_op jit(solution)/shard_map/all_gather | solution.py:40
  177.3 3.7 %reduce_sum.62 = bf16[32,8192]{1,0:T(8,128)(2,1)} reduce(bf16[8,32,8192]{2,1,0:T(8,128)(2,1)} %all-gather.3.cloned.1.call-done, bf16[]{:T(256)} %constant.58.clone.1), dimensions={0}, to_apply=%region_5.6 | reduce | flops 1835008 | bytes 4718594 | tf_op jit(solution)/shard_map/reduce_sum | solution.py:40
  183.8 2.6 copy.38
  188.0 3.2 gather_fusion.2
  191.2 61.2 %all_to_all.22 = bf16[32,8,4096]{2,1,0:T(8,128)(2,1)} all-to-all(bf16[32,8,4096]{2,1,0:T(8,128)(2,1)} %bitcast.69), channel_id=1, replica_groups=mesh['row'=32,'col'=8] {'row'}, dimensions={0} | all-to-all | bytes 4194304 | tf_op jit(solution)/shard_map/all_to_all | solution.py:33
  252.4 9.4 %reshape.294 = bf16[256,128,32]{2,1,0:T(8,128)(2,1)} reshape(bf16[32,8,4096]{2,1,0:T(8,128)(2,1)} %all_to_all.22) | data formatting | bytes 4194304 | tf_op jit(solution)/shard_map/reshape | solution.py:34
  261.8 7.9 %copy.40 = bf16[256,128,32]{1,2,0:T(8,128)(2,1)} copy(bf16[256,128,32]{2,1,0:T(8,128)(2,1)} %reshape.294) | data formatting | bytes 4194304 | tf_op jit(solution)/shard_map/reshape | solution.py:34
  269.7 3.3 %pad_maximum_fusion.1 = bf16[320,128,32]{1,2,0:T(8,128)(2,1)} fusion(bf16[256,128,32]{1,2,0:T(8,128)(2,1)} %copy.40, bf16[64,128,32]{1,2,0:T(8,128)(2,1)S(1)} %fusion.2), kind=kLoop, calls=%fused_computation.8 | loop fusion | flops 1310720 | bytes 5242880 | tf_op jit(solution)/shard_map/concatenate | solution.py:34
  273.0 4.9 %gather_fusion.3 = bf16[512,128,32]{1,2,0:T(8,128)(2,1)} fusion(bf16[320,128,32]{1,2,0:T(8,128)(2,1)} %pad_maximum_fusion.1, s32[1024]{0:T(1024)S(1)} %pad_clamp_fusion), kind=kCustom, calls=%fused_computation.3 | custom fusion | bytes 8390656 | tf_op jit(solution)/shard_map/gather | solution.py:35
  277.9 3.1 bitcast_reduce_fusion
  283.5 30.1 %all-gather.5.cloned.1.call-done = bf16[8,32,8192]{2,1,0:T(8,128)(2,1)} async-done(((bf16[1,32,8192]{2,1,0:T(8,128)(2,1)}), bf16[8,32,8192]{2,1,0:T(8,128)(2,1)}) %all-gather.5.cloned.1.call-update) | async-done | bytes 4194320 | tf_op jit(solution)/shard_map/all_gather | solution.py:40
  313.6 3.7 %reduce_sum.64 = bf16[32,8192]{1,0:T(8,128)(2,1)} reduce(bf16[8,32,8192]{2,1,0:T(8,128)(2,1)} %all-gather.5.cloned.1.call-done, bf16[]{:T(256)} %constant.58.clone.1), dimensions={0}, to_apply=%region_7.8 | reduce | flops 1835008 | bytes 4718594 | tf_op jit(solution)/shard_map/reduce_sum | solution.py:40
  317.3 2.5 multiply_subtract_fusion
  (48 shorter events, 18.0 us)
Async XLA Ops:
  7.2 37.5 %copy-start = (bf16[8192,128]{1,0:T(8,128)(2,1)S(1)}, bf16[8192,128]{1,0:T(8,128)(2,1)}, u32[]{:S(2)}) copy-start(bf16[8192,128]{1,0:T(8,128)(2,1)} %param.4) | copy-start | bytes 6291460
  10.0 34.7 %copy-start.1 = (f32[32,8192]{1,0:T(8,128)S(1)}, f32[32,8192]{1,0:T(8,128)}, u32[]{:S(2)}) copy-start(f32[32,8192]{1,0:T(8,128)} %param.6) | copy-start | bytes 3145732
  10.1 34.7 %copy-start.5 = (f32[8192]{0:T(1024)S(1)}, f32[8192]{0:T(1024)}, u32[]{:S(2)}) copy-start(f32[8192]{0:T(1024)} %param.5) | copy-start | bytes 98308
  33.0 20.3 %all-to-all-start = ((s32[32,1,8]{2,1,0:T(1,128)}), s32[32,1,8]{2,1,0:T(1,128)S(1)}, u32[]{:S(2)}, u32[]{:S(2)}) async-start(s32[32,1,8]{2,1,0:T(1,128)} %copy.31), calls=%async_computation | async-start | bytes 32768 | tf_op jit(solution)/shard_map/all_to_all | solution.py:24
  56.6 56.9 %all-to-all-start.1 = ((bf16[32,8,4096]{2,1,0:T(8,128)(2,1)}), bf16[32,8,4096]{2,1,0:T(8,128)(2,1)}, u32[]{:S(2)}, u32[]{:S(2)}) async-start(bf16[32,8,4096]{2,1,0:T(8,128)(2,1)} %bitcast.68), calls=%async_computation.1 | async-start | bytes 4194304 | tf_op jit(solution)/shard_map/all_to_all | solution.py:33
  64.6 112.6 %all-gather.3.cloned.1.call-start = ((), (), s32[]{:S(2)}) async-start(), calls=%async_computation.3 | async-start | bytes 4718592 | tf_op jit(solution)/shard_map/all_gather | solution.py:40
  122.8 8.0 %copy-start.4 = (bf16[64,128,32]{1,2,0:T(8,128)(2,1)S(1)}, bf16[64,128,32]{1,2,0:T(8,128)(2,1)}, u32[]{:S(2)}) copy-start(bf16[64,128,32]{1,2,0:T(8,128)(2,1)} %fusion) | copy-start | bytes 1572868
  144.6 36.4 %copy-start.2 = (f32[32,8192]{1,0:T(8,128)S(1)}, f32[32,8192]{1,0:T(8,128)}, u32[]{:S(2)}) copy-start(f32[32,8192]{1,0:T(8,128)} %param.6) | copy-start | bytes 3145732
  144.6 169.0 %all-gather.5.cloned.1.call-start = ((), (), s32[]{:S(2)}) async-start(), calls=%async_computation.4 | async-start | bytes 4718592 | tf_op jit(solution)/shard_map/all_gather | solution.py:40
  283.5 33.9 %copy-start.3 = (f32[32,8192]{1,0:T(8,128)S(1)}, f32[32,8192]{1,0:T(8,128)}, u32[]{:S(2)}) copy-start(f32[32,8192]{1,0:T(8,128)} %param.6) | copy-start | bytes 3145732
Sparse Core Ops, SparseCore 0:
  144.7 32.4 all-gather.2
  283.6 29.9 all-gather.4
